TPU v7x, 256 devices: a whole 4x4x8 slice. The times are simulated.
256 devices in a mesh: vp: 128 (over y, x, z), op: 2 (over core).
Axes of the slice: x: 4, y: 4, z: 8, core: 2. Of those that a mesh axis runs over, the one named last changes fastest.
Arguments:
- multipliers: bfloat16 [2048, 131072], P('op', 'vp'), may hold values from -6 to 6
- integrals: bfloat16 [131072, 1024], P('vp'), may hold values from -0.0625 to 0.0625
- amplitudes: bfloat16 [2048, 131072], P('op', 'vp'), may hold values from -0.09375 to 0.09375
- slab_multipliers: bfloat16 [1024, 2048], P('vp', 'op'), may hold values from -6 to 6
- slab_amplitudes: bfloat16 [1024, 2048], P('vp', 'op'), may hold values from -0.09375 to 0.09375
- residual_rest: bfloat16 [1024, 2048], P('vp', 'op'), may hold values from -6 to 6
- occupied_energy: bfloat16 [2048], P('op'), may hold values from -2.5 to -0.5
- virtual_energy: bfloat16 [1024], P('vp'), may hold values from 1 to 4
Outputs:
- updated_multipliers: bfloat16 [1024, 2048], P('vp', 'op')
- pair_density: bfloat16 [1024, 131072], P('op', 'vp')
All inputs are finite; a program needn't handle non-finite values.
Results may differ from a plain program's by a relative error of at most 0.004.
Values may be sent and summed in bfloat16 or wider, within the bound.
A program may use at most 64 MiB of HBM per device.

v0:
```python
import jax
import jax.numpy as jnp
from jax import lax
from jax.sharding import PartitionSpec as P


def renew_slab(current, ladder, rest, virtual, occupied):
    divisor = virtual.astype(jnp.float32)[:, None] - occupied.astype(jnp.float32)[None, :]
    renewed = current.astype(jnp.float32) + (ladder + rest.astype(jnp.float32)) / divisor
    return renewed.astype(jnp.bfloat16)


def local(
    multipliers,
    integrals,
    amplitudes,
    slab_multipliers,
    slab_amplitudes,
    residual_rest,
    occupied_energy,
    virtual_energy,
):
    rows_dev = slab_multipliers.shape[0]
    every_old, every_amp, every_rest, every_virtual = (
        lax.all_gather(slab_multipliers, "vp", axis=0, tiled=True),
        lax.all_gather(slab_amplitudes, "vp", axis=0, tiled=True),
        lax.all_gather(residual_rest, "vp", axis=0, tiled=True),
        lax.all_gather(virtual_energy, "vp", axis=0, tiled=True),
    )
    ladder = lax.psum(
        lax.dot_general(
            integrals, multipliers, (((0,), (1,)), ((), ())), preferred_element_type=jnp.float32
        ),
        "vp",
    )
    every_new = renew_slab(every_old, ladder, every_rest, every_virtual, occupied_energy)
    renewed = lax.dynamic_slice_in_dim(every_new, lax.axis_index("vp") * rows_dev, rows_dev, 0)
    first = jnp.dot(every_new, amplitudes, preferred_element_type=jnp.float32)
    density = lax.psum_scatter(
        first + jnp.dot(every_amp, multipliers, preferred_element_type=jnp.float32),
        "op",
        scatter_dimension=0,
        tiled=True,
    )
    return (renewed, density.astype(jnp.bfloat16))


def solution(mesh):
    placed = (
        P("op", "vp"),
        P("vp", None),
        P("op", "vp"),
        P("vp", "op"),
        P("vp", "op"),
        P("vp", "op"),
        P("op"),
        P("vp"),
    )
    return jax.shard_map(
        local, mesh=mesh, in_specs=placed, out_specs=(P("vp", "op"), P("op", "vp")), check_vma=False
    )
```

profile of v0, /device:TPU:1, one launch (start us, length us, event | category | flops | bytes accessed | tf_op | source)
XLA Modules:
  0.0 628.6 jit_solution(17845143190247630263)
XLA Ops:
  7.2 0.0 copy-start
  7.2 0.0 all-gather.4.cloned.1.call-start
  7.2 0.7 all-gather.4.cloned.1.call-update
  7.9 0.0 all-gather.6.cloned.1.call-start
  8.0 0.7 all-gather.6.cloned.1.call-update
  8.7 0.0 all-reduce.3.cloned.1.call-start
  8.7 0.1 copy-done
  8.8 5.9 fusion
  14.7 0.0 copy-start.5
  14.7 0.0 copy-start.4
  14.7 0.0 copy-start.2
  14.7 0.0 all-reduce.3.cloned.1.call-update
  14.7 0.0 all-gather.8.cloned.1.call-start
  14.8 0.5 all-gather.8.cloned.1.call-update
  15.3 0.0 reduce-scatter.2.cloned.1.call-start
  15.4 0.0 copy-done.5
  15.4 0.6 dynamic-slice
  16.6 0.0 copy-done.4
  16.6 0.2 dynamic-update-slice
  16.9 299.1 %all-reduce = bf16[1024]{0:T(1024)(128)(2,1)S(1)} all-reduce(bf16[1024]{0:T(1024)(128)(2,1)S(1)} %dynamic-update-slice), channel_id=1, replica_groups=mesh['vp'=128,'op'=2] {'vp'}, use_global_device_ids=true, to_apply=%add | all-reduce | flops 1024 | bytes 4096
  316.0 0.0 copy-done.2
  316.0 0.0 all-gather.4.cloned.1.call-done
  316.0 0.0 all-gather.6.cloned.1.call-done
  316.0 162.0 %all-reduce.3.cloned.1.call-done = f32[1024,1024]{1,0:T(8,128)} async-done(((f32[1024,1024]{1,0:T(8,128)}), f32[1024,1024]{1,0:T(8,128)}) %all-reduce.3.cloned.1.call-update) | async-done | bytes 4194320 | tf_op jit(solution)/shard_map/psum | solution.py:30
  478.1 0.0 copy-start.3
  478.1 4.6 add_convert_fusion
  482.7 0.0 copy-start.1
  482.7 1.3 copy-done.1
  484.0 0.0 copy-done.3
  484.0 4.3 fusion.1
  488.3 104.1 %all-gather.8.cloned.1.call-done = bf16[1024,1024]{1,0:T(8,128)(2,1)} async-done(((bf16[8,1024]{1,0:T(8,128)(2,1)}), bf16[1024,1024]{1,0:T(8,128)(2,1)}) %all-gather.8.cloned.1.call-update) | async-done | bytes 2097168 | tf_op jit(solution)/shard_map/all_gather | solution.py:26
  592.5 7.1 %convolution_add_fusion = f32[1024,1024]{1,0:T(8,128)} fusion(f32[1024,1024]{1,0:T(8,128)} %fusion.1, bf16[1024,1024]{1,0:T(8,128)(2,1)} %all-gather.8.cloned.1.call-done, bf16[1024,1024]{1,0:T(8,128)(2,1)S(1)} %copy-done), kind=kOutput, calls=%fused_computation.1 | convolution fusion | flops 2148532224 | bytes 12582912 | tf_op jit(solution)/shard_map/dot_general | solution.py:40
  599.6 0.0 reduce-scatter.2.cloned.1.call-update
  599.6 1.3 constant_dynamic-slice_fusion
  600.9 18.4 %reduce-scatter.2.cloned.1.call-done = f32[512,1024]{1,0:T(8,128)} async-done(((f32[1024,1024]{1,0:T(8,128)}), f32[512,1024]{1,0:T(8,128)}) %reduce-scatter.2.cloned.1.call-update) | async-done | bytes 2097168 | tf_op jit(solution)/shard_map/reduce_scatter | solution.py:39
  619.3 2.7 convert_element_type.23
  (3 shorter events, 0.0 us)
Async XLA Ops:
  7.2 1.6 copy-start
  7.2 308.8 %all-gather.4.cloned.1.call-start = ((), (), s32[]{:S(2)}) async-start(), calls=%async_computation.1 | async-start | bytes 2113536 | tf_op jit(solution)/shard_map/all_gather | solution.py:25
  7.9 308.1 %all-gather.6.cloned.1.call-start = ((), (), s32[]{:S(2)}) async-start(), calls=%async_computation.3 | async-start | bytes 2113536 | tf_op jit(solution)/shard_map/all_gather | solution.py:27
  8.7 469.4 %all-reduce.3.cloned.1.call-start = ((), (), s32[]{:S(2)}) async-start(), calls=%async_computation.2 | async-start | bytes 8388608 | tf_op jit(solution)/shard_map/psum | solution.py:30
  14.7 0.7 copy-start.5
  14.7 1.9 copy-start.4
  14.7 301.3 %copy-start.2 = (bf16[1024]{0:T(1024)(128)(2,1)S(1)}, bf16[1024]{0:T(1024)(128)(2,1)}, u32[]{:S(2)}) copy-start(bf16[1024]{0:T(1024)(128)(2,1)} %param.14) | copy-start | bytes 6148
  14.7 577.7 %all-gather.8.cloned.1.call-start = ((), (), s32[]{:S(2)}) async-start(), calls=%async_computation.4 | async-start | bytes 2113536 | tf_op jit(solution)/shard_map/all_gather | solution.py:26
  15.3 604.0 %reduce-scatter.2.cloned.1.call-start = ((), (), s32[]{:S(2)}) async-start(), calls=%async_computation.5 | async-start | bytes 6291456 | tf_op jit(solution)/shard_map/reduce_scatter | solution.py:39
  478.1 6.0 copy-start.3
  482.7 1.3 copy-start.1
Sparse Core Ops, SparseCore 0:
  11.6 113.6 all-gather.3
  128.9 111.2 all-gather.5
  245.6 232.4 all-reduce.2
  482.1 110.2 all-gather.7
  599.7 19.5 reduce-scatter.1
where the time goes:
time: 629 us
  blocking collectives  299 us (48%)
  waiting for transfers between devices  287 us (46%)
  matrix products  17.3 us (3%)
  between operations  14.5 us (2%)
  other arithmetic  7.38 us (1%)
    unnamed x1, blocking collectives  299 us
    psum x1, waiting for transfers between devices, local(): lax.psum(lax.dot_general(integrals, multipliers, (((0,), (1,)), ((), ()))...  162 us
    all_gather x1, waiting for transfers between devices, local(): lax.all_gather(slab_amplitudes, 'vp', axis=0, tiled=True)  104 us
    reduce_scatter x1, waiting for transfers between devices, local(): lax.psum_scatter(first + jnp.dot(every_amp, multipliers, preferred_elemen...  18.4 us
  transfers between devices with their start and end apart: 5, of which 3 were waited for; matrix products, arithmetic and copies ran while one was open for 3% of the time, Pallas kernels for 0%

commit v1 on v0

--- a/solution.py
+++ b/solution.py
@@ -20,21 +20,19 @@
     occupied_energy,
     virtual_energy,
 ):
-    rows_dev = slab_multipliers.shape[0]
-    every_old, every_amp, every_rest, every_virtual = (
-        lax.all_gather(slab_multipliers, "vp", axis=0, tiled=True),
-        lax.all_gather(slab_amplitudes, "vp", axis=0, tiled=True),
-        lax.all_gather(residual_rest, "vp", axis=0, tiled=True),
-        lax.all_gather(virtual_energy, "vp", axis=0, tiled=True),
-    )
-    ladder = lax.psum(
+    every_amp = lax.all_gather(slab_amplitudes, "vp", axis=0, tiled=True)
+    ladder = lax.psum_scatter(
         lax.dot_general(
             integrals, multipliers, (((0,), (1,)), ((), ())), preferred_element_type=jnp.float32
         ),
         "vp",
+        scatter_dimension=0,
+        tiled=True,
     )
-    every_new = renew_slab(every_old, ladder, every_rest, every_virtual, occupied_energy)
-    renewed = lax.dynamic_slice_in_dim(every_new, lax.axis_index("vp") * rows_dev, rows_dev, 0)
+    renewed = renew_slab(
+        slab_multipliers, ladder, residual_rest, virtual_energy, occupied_energy
+    )
+    every_new = lax.all_gather(renewed, "vp", axis=0, tiled=True)
     first = jnp.dot(every_new, amplitudes, preferred_element_type=jnp.float32)
     density = lax.psum_scatter(
         first + jnp.dot(every_amp, multipliers, preferred_element_type=jnp.float32),

time: 629 us -> 980 us (1.56)
  waiting for transfers between devices: 287 us -> 940 us
  blocking collectives: 299 us -> 0 us
    reduce_scatter x0 -> x1, waiting for transfers between devices: none -> 599 us  [local(): lax.psum_scatter(lax.dot_general(integrals, multipliers, (((0,), (1,)), (...]
    unnamed x1 -> x0, blocking collectives: 299 us -> none
    all_gather x3 -> x2, waiting for transfers between devices: 104 us -> 320 us  [the longest x1 211 us: local(): every_new = lax.all_gather(renewed, 'vp', axis=0, tiled=True)]
    psum x1 -> x0, waiting for transfers between devices: 162 us -> none  [local(): lax.psum(lax.dot_general(integrals, multipliers, (((0,), (1,)), ((), ()))...]
  transfers between devices with their start and end apart: 5 -> 4, of which waited for: 3 -> 4; matrix products, arithmetic and copies ran while one was open for 3% -> 1% of each run, Pallas kernels for 0% -> 0%
where the time goes in v1:
time: 980 us
  waiting for transfers between devices  940 us (96%)
  matrix products  19.5 us (2%)
  between operations  13.8 us (1%)
    reduce_scatter x1, waiting for transfers between devices, local(): lax.psum_scatter(lax.dot_general(integrals, multipliers, (((0,), (1,)), (...  599 us
    all_gather x1, waiting for transfers between devices, local(): every_new = lax.all_gather(renewed, 'vp', axis=0, tiled=True)  211 us
    all_gather x1, waiting for transfers between devices, local(): every_amp = lax.all_gather(slab_amplitudes, 'vp', axis=0, tiled=True)  109 us
    reduce_scatter x1, waiting for transfers between devices, local(): lax.psum_scatter(first + jnp.dot(every_amp, multipliers, preferred_elemen...  19.7 us
  transfers between devices with their start and end apart: 4, of which 4 were waited for; matrix products, arithmetic and copies ran while one was open for 1% of the time, Pallas kernels for 0%

profile of v1, /device:TPU:1, one launch (start us, length us, event | category | flops | bytes accessed | tf_op | source)
XLA Modules:
  0.0 979.7 jit_solution(14029805148168330737)
XLA Ops:
  7.2 0.0 copy-start
  7.2 0.0 reduce-scatter.3.cloned.1.call-start
  7.2 1.5 copy-done
  8.8 5.9 fusion
  14.7 0.0 copy-start.3
  14.7 0.0 copy-start.4
  14.7 0.0 copy-start.1
  14.7 0.0 copy-start.2
  14.7 0.0 reduce-scatter.3.cloned.1.call-update
  14.7 0.0 all-gather.3.cloned.1.call-start
  14.8 0.6 copy-done.3
  15.4 0.0 copy-done.4
  15.4 599.1 %reduce-scatter.3.cloned.1.call-done = f32[8,1024]{1,0:T(8,128)} async-done(((f32[1024,1024]{1,0:T(8,128)}), f32[8,1024]{1,0:T(8,128)}) %reduce-scatter.3.cloned.1.call-update) | async-done | bytes 32784 | tf_op jit(solution)/shard_map/reduce_scatter | solution.py:24
  614.5 0.0 copy-done.1
  614.5 0.0 copy-done.2
  614.5 1.4 add_convert_fusion
  616.0 0.0 all-gather.3.cloned.1.call-update
  616.0 0.0 all-gather.5.cloned.1.call-start
  616.0 0.7 all-gather.5.cloned.1.call-update
  616.7 0.0 reduce-scatter.5.cloned.1.call-start
  616.8 211.2 %all-gather.3.cloned.1.call-done = bf16[1024,1024]{1,0:T(8,128)(2,1)} async-done(((bf16[8,1024]{1,0:T(8,128)(2,1)}), bf16[1024,1024]{1,0:T(8,128)(2,1)}) %all-gather.3.cloned.1.call-update) | async-done | bytes 2097168 | tf_op jit(solution)/shard_map/all_gather | solution.py:35
  828.0 6.5 fusion.1
  834.5 109.1 %all-gather.5.cloned.1.call-done = bf16[1024,1024]{1,0:T(8,128)(2,1)} async-done(((bf16[8,1024]{1,0:T(8,128)(2,1)}), bf16[1024,1024]{1,0:T(8,128)(2,1)}) %all-gather.5.cloned.1.call-update) | async-done | bytes 2097168 | tf_op jit(solution)/shard_map/all_gather | solution.py:23
  943.5 7.1 convolution_add_fusion
  950.6 0.0 reduce-scatter.5.cloned.1.call-update
  950.7 19.7 %reduce-scatter.5.cloned.1.call-done = f32[512,1024]{1,0:T(8,128)} async-done(((f32[1024,1024]{1,0:T(8,128)}), f32[512,1024]{1,0:T(8,128)}) %reduce-scatter.5.cloned.1.call-update) | async-done | bytes 2097168 | tf_op jit(solution)/shard_map/reduce_scatter | solution.py:37
  970.4 2.7 convert_element_type.23
  (2 shorter events, 0.0 us)
Async XLA Ops:
  7.2 1.6 copy-start
  7.2 607.3 %reduce-scatter.3.cloned.1.call-start = ((), (), s32[]{:S(2)}) async-start(), calls=%async_computation.2 | async-start | bytes 4227072 | tf_op jit(solution)/shard_map/reduce_scatter | solution.py:24
  14.7 0.7 copy-start.3
  14.7 0.7 copy-start.4
  14.7 599.8 %copy-start.1 = (bf16[8,1024]{1,0:T(8,128)(2,1)S(1)}, bf16[8,1024]{1,0:T(8,128)(2,1)}, u32[]{:S(2)}) copy-start(bf16[8,1024]{1,0:T(8,128)(2,1)} %param.13) | copy-start | bytes 49156
  14.7 599.8 %copy-start.2 = (bf16[8,1024]{1,0:T(8,128)(2,1)S(1)}, bf16[8,1024]{1,0:T(8,128)(2,1)}, u32[]{:S(2)}) copy-start(bf16[8,1024]{1,0:T(8,128)(2,1)} %param.11) | copy-start | bytes 49156
  14.7 813.2 %all-gather.3.cloned.1.call-start = ((), (), s32[]{:S(2)}) async-start(), calls=%async_computation.3 | async-start | bytes 2113536 | tf_op jit(solution)/shard_map/all_gather | solution.py:35
  616.0 327.5 %all-gather.5.cloned.1.call-start = ((), (), s32[]{:S(2)}) async-start(), calls=%async_computation.4 | async-start | bytes 2113536 | tf_op jit(solution)/shard_map/all_gather | solution.py:23
  616.7 353.7 %reduce-scatter.5.cloned.1.call-start = ((), (), s32[]{:S(2)}) async-start(), calls=%async_computation.5 | async-start | bytes 6291456 | tf_op jit(solution)/shard_map/reduce_scatter | solution.py:37
Sparse Core Ops, SparseCore 0:
  14.8 599.6 reduce-scatter.2
  619.3 208.6 all-gather.2
  832.2 111.3 all-gather.4
  950.8 19.5 reduce-scatter.4

commit v2 on v1

v2 whole, which is shorter than its diff:
```python
import functools

import jax
import jax.numpy as jnp
from jax import lax
from jax.experimental import pallas as pl
from jax.experimental.pallas import tpu as pltpu
from jax.sharding import PartitionSpec as P

F32 = jnp.float32
BF16 = jnp.bfloat16


def kernel(
    dims,
    mul_hbm, int_hbm, amp_hbm, slab_ref, slab_amp_ref, rest_ref, div_ref,
    new_ref, den_ref,
    mul, integ, amp, lad, got1a, got1b, sum1, got2, sum2, got3,
    new_z, new_all, am_z, am_all, acc, swap_out, swap_in,
    load_sem,
    s1a, r1a, s1b, r1b, s2, r2, s3, r3,
    nz_s, nz_r, n2_s, n2_r, n3_s, n3_r,
    az_s, az_r, a2_s, a2_r, a3_s, a3_r,
    sw_s, sw_r,
):
    Y, X, Z = dims
    v = lax.axis_index("vp")
    c = lax.axis_index("op")
    y = v // (X * Z)
    x = lax.rem(v // Z, X)
    z = lax.rem(v, Z)
    B = 8 * Z
    W = lad.shape[-1]

    def peer_y(k):
        return lax.rem(y + k, Y)

    def peer_x(k):
        return lax.rem(x + k, X)

    def peer_z(k):
        return lax.rem(z + k, Z)

    def at_y(i):
        return {"vp": (i * X + x) * Z + z}

    def at_x(i):
        return {"vp": (y * X + i) * Z + z}

    def at_z(i):
        return {"vp": (y * X + x) * Z + i}

    other = {"op": 1 - c}

    def remote(src, dst, ss, rs, device):
        return pltpu.make_async_remote_copy(
            src_ref=src, dst_ref=dst, send_sem=ss, recv_sem=rs,
            device_id=device, device_id_type=pl.DeviceIdType.MESH,
        )

    load_m = pltpu.make_async_copy(mul_hbm, mul, load_sem.at[0])
    load_i = pltpu.make_async_copy(int_hbm, integ, load_sem.at[1])
    load_a = pltpu.make_async_copy(amp_hbm, amp, load_sem.at[2])
    load_m.start()
    load_i.start()
    load_a.start()

    barrier = pltpu.get_barrier_semaphore()
    greet = (
        [at_y(peer_y(k)) for k in range(1, Y)]
        + [at_x(peer_x(k)) for k in range(1, X)]
        + [at_z(peer_z(k)) for k in range(1, Z)]
        + [other]
    )
    for device in greet:
        pl.semaphore_signal(barrier, inc=1, device_id=device, device_id_type=pl.DeviceIdType.MESH)

    rows_z = pl.ds(pl.multiple_of(z * 8, 8), 8)
    am_z[rows_z, :] = slab_amp_ref[...].astype(F32)
    load_m.wait()
    load_i.wait()
    pl.semaphore_wait(barrier, len(greet))

    def spread_z(buf, ss, rs):
        out = []
        for k in range(1, Z):
            d = remote(
                buf.at[rows_z, :], buf.at[rows_z, :], ss.at[k - 1], rs.at[Z - 1 - k],
                at_z(peer_z(k)),
            )
            d.start()
            out.append(d)
        return out

    def spread_own(buf_z, full, ss2, rs2, ss3, rs3):
        out = []
        full[0, y, x] = buf_z[:, :W].astype(BF16)
        full[1, y, x] = buf_z[:, W:].astype(BF16)
        for k in range(1, Y):
            here = full.at[0, y, x]
            d = remote(here, here, ss2.at[0, k - 1], rs2.at[0, Y - 1 - k], at_y(peer_y(k)))
            d.start()
            out.append(d)
            here = full.at[1, y, x]
            d = remote(here, here, ss2.at[1, k - 1], rs2.at[1, X - 1 - k], at_x(peer_x(k)))
            d.start()
            out.append(d)
        for k in range(1, Y):
            here = full.at[0, y, x]
            d = remote(here, here, ss3.at[0, k - 1, 0], rs3.at[0, X - 1 - k, 0], at_x(peer_x(k)))
            d.start()
            out.append(d)
            here = full.at[1, y, x]
            d = remote(here, here, ss3.at[1, k - 1, 0], rs3.at[1, Y - 1 - k, 0], at_y(peer_y(k)))
            d.start()
            out.append(d)
        return out

    def spread_got(full, got2_d, ss3, rs3):
        out = []
        for i in range(Y - 1):
            got2_d[0][i].wait_recv()
            here = full.at[0, peer_y(i + 1), x]
            for k in range(1, X):
                d = remote(
                    here, here, ss3.at[0, k - 1, i + 1], rs3.at[0, X - 1 - k, i + 1],
                    at_x(peer_x(k)),
                )
                d.start()
                out.append(d)
            got2_d[1][i].wait_recv()
            here = full.at[1, y, peer_x(i + 1)]
            for k in range(1, Y):
                d = remote(
                    here, here, ss3.at[1, k - 1, i + 1], rs3.at[1, Y - 1 - k, i + 1],
                    at_y(peer_y(k)),
                )
                d.start()
                out.append(d)
        return out

    def arrivals_z(buf, ss, rs):
        out = []
        for i in range(Z - 1):
            rows = pl.ds(pl.multiple_of(peer_z(i + 1) * 8, 8), 8)
            out.append(remote(buf.at[rows, :], buf.at[rows, :], ss.at[i], rs.at[i], at_z(peer_z(i + 1))))
        return out

    def arrivals_2(full, ss, rs):
        a = []
        b = []
        for i in range(Y - 1):
            here = full.at[0, peer_y(i + 1), x]
            a.append(remote(here, here, ss.at[0, i], rs.at[0, i], at_y(peer_y(i + 1))))
        for i in range(X - 1):
            here = full.at[1, y, peer_x(i + 1)]
            b.append(remote(here, here, ss.at[1, i], rs.at[1, i], at_x(peer_x(i + 1))))
        return a, b

    def arrivals_3(full, ss, rs):
        out = []
        for j in range(Y):
            for i in range(X - 1):
                here = full.at[0, peer_y(j), peer_x(i + 1)]
                out.append(remote(here, here, ss.at[0, i, j], rs.at[0, i, j], at_x(peer_x(i + 1))))
                here = full.at[1, peer_y(i + 1), peer_x(j)]
                out.append(remote(here, here, ss.at[1, i, j], rs.at[1, i, j], at_y(peer_y(i + 1))))
        return out

    sent = []
    sent += spread_z(am_z, az_s, az_r)

    for n in range(Y):
        k = n + 1
        yb = peer_y(k)
        cols = pl.ds(pl.multiple_of(yb * (X * B), X * B), X * B)
        part = lax.dot_general(
            integ[:, cols], mul[...], (((0,), (1,)), ((), ())), preferred_element_type=F32
        )
        lad[0, yb] = part[:, :W].astype(BF16).reshape(X, B, W)
        lad[1, yb] = part[:, W:].astype(BF16).reshape(X, B, W)
        if k < Y:
            d = remote(lad.at[1, yb], got1b.at[Y - 1 - k], s1b.at[k - 1], r1b.at[Y - 1 - k], at_y(yb))
            d.start()
            sent.append(d)
        for kx in range(1, X):
            xb = peer_x(kx)
            d = remote(
                lad.at[0, yb, xb], got1a.at[X - 1 - kx, yb],
                s1a.at[kx - 1, n], r1a.at[X - 1 - kx, n], at_x(xb),
            )
            d.start()
            sent.append(d)

    for d in arrivals_z(am_z, az_s, az_r):
        d.wait_recv()
    sent += spread_own(am_z, am_all, a2_s, a2_r, a3_s, a3_r)

    for n in range(Y):
        k = n + 1
        yb = peer_y(k)
        for i in range(X - 1):
            remote(
                lad.at[0, yb, x], got1a.at[i, yb], s1a.at[i, n], r1a.at[i, n], at_x(peer_x(i + 1))
            ).wait_recv()
        total = lad[0, yb, x].astype(F32)
        for i in range(X - 1):
            total = total + got1a[i, yb].astype(F32)
        if k < Y:
            sum1[0, n] = total.astype(BF16)
            d = remote(sum1.at[0, n], got2.at[0, Y - 1 - k], s2.at[0, n], r2.at[0, Y - 1 - k], at_y(yb))
            d.start()
            sent.append(d)
        else:
            sum2[:, :W] = total
    for i in range(Y - 1):
        remote(
            lad.at[1, y], got1b.at[i], s1b.at[i], r1b.at[i], at_y(peer_y(i + 1))
        ).wait_recv()
    for n in range(X):
        k = n + 1
        xb = peer_x(k)
        total = lad[1, y, xb].astype(F32)
        for i in range(Y - 1):
            total = total + got1b[i, xb].astype(F32)
        if k < X:
            sum1[1, n] = total.astype(BF16)
            d = remote(sum1.at[1, n], got2.at[1, X - 1 - k], s2.at[1, n], r2.at[1, X - 1 - k], at_x(xb))
            d.start()
            sent.append(d)
        else:
            sum2[:, W:] = total

    for h in range(2):
        cols = slice(h * W, (h + 1) * W)
        for i in range(got2.shape[1]):
            device = at_y(peer_y(i + 1)) if h == 0 else at_x(peer_x(i + 1))
            remote(sum1.at[h, i], got2.at[h, i], s2.at[h, i], r2.at[h, i], device).wait_recv()
        total = sum2[:, cols]
        for i in range(got2.shape[1]):
            total = total + got2[h, i].astype(F32)
        sum2[:, cols] = total
    for k in range(1, Z):
        zb = peer_z(k)
        rows = pl.ds(pl.multiple_of(zb * 8, 8), 8)
        d = remote(sum2.at[rows, :], got3.at[Z - 1 - k], s3.at[k - 1], r3.at[Z - 1 - k], at_z(zb))
        d.start()
        sent.append(d)

    for i in range(Z - 1):
        remote(
            sum2.at[rows_z, :], got3.at[i], s3.at[i], r3.at[i], at_z(peer_z(i + 1))
        ).wait_recv()
    ladder = sum2[rows_z, :]
    for i in range(Z - 1):
        ladder = ladder + got3[i]
    renewed = slab_ref[...].astype(F32) + (ladder + rest_ref[...].astype(F32)) / div_ref[...]
    renewed = renewed.astype(BF16)
    new_ref[...] = renewed
    new_z[rows_z, :] = renewed.astype(F32)
    sent += spread_z(new_z, nz_s, nz_r)

    sent += spread_got(am_all, arrivals_2(am_all, a2_s, a2_r), a3_s, a3_r)

    for d in arrivals_z(new_z, nz_s, nz_r):
        d.wait_recv()
    sent += spread_own(new_z, new_all, n2_s, n2_r, n3_s, n3_r)
    sent += spread_got(new_all, arrivals_2(new_all, n2_s, n2_r), n3_s, n3_r)

    for d in arrivals_3(am_all, a3_s, a3_r):
        d.wait_recv()
    R = X * B
    first = 1 - c

    def block_of(t):
        return jnp.where(t < Y // 2, first * (Y // 2) + t, c * (Y // 2) + t - Y // 2)

    @pl.loop(0, Y)
    def _(t):
        yb = block_of(t)
        acc[t] = jnp.dot(
            am_all[0, yb].reshape(R, W), mul[:W, :], preferred_element_type=F32
        ) + jnp.dot(am_all[1, yb].reshape(R, W), mul[W:, :], preferred_element_type=F32)

    load_a.wait()
    for d in arrivals_3(new_all, n3_s, n3_r):
        d.wait_recv()

    def density(t):
        yb = block_of(t)
        return (
            acc[t]
            + jnp.dot(new_all[0, yb].reshape(R, W), amp[:W, :], preferred_element_type=F32)
            + jnp.dot(new_all[1, yb].reshape(R, W), amp[W:, :], preferred_element_type=F32)
        )

    swaps = []
    for t in range(Y // 2):
        swap_out[t] = density(t).astype(swap_out.dtype)
        d = remote(swap_out.at[t], swap_in.at[t], sw_s.at[t], sw_r.at[t], other)
        d.start()
        swaps.append(d)
    for t in range(Y // 2):
        acc[Y // 2 + t] = density(Y // 2 + t)
    for t in range(Y // 2):
        swaps[t].wait_recv()
        den_ref[pl.ds(t * R, R), :] = (acc[Y // 2 + t] + swap_in[t].astype(F32)).astype(BF16)
    for d in sent + swaps:
        d.wait_send()


def local(dims, mul, integ, amp, slab, slab_amp, rest, occupied, virtual):
    Y, X, Z = dims
    B = 8 * Z
    R = Y * X * B
    p, q = mul.shape
    W = p // 2
    divisor = virtual.astype(F32)[:, None] - occupied.astype(F32)[None, :]
    dma = pltpu.SemaphoreType.DMA
    vmem = pl.BlockSpec(memory_space=pltpu.VMEM)
    hbm = pl.BlockSpec(memory_space=pl.ANY)
    gather_sems = [
        dma((Z - 1,)), dma((Z - 1,)),
        dma((2, Y - 1)), dma((2, Y - 1)),
        dma((2, Y - 1, Y)), dma((2, Y - 1, Y)),
    ]
    scratch = [
        pltpu.VMEM((p, q), BF16),
        pltpu.VMEM((q, R), BF16),
        pltpu.VMEM((p, q), BF16),
        pltpu.VMEM((2, Y, X, B, W), BF16),
        pltpu.VMEM((X - 1, Y, B, W), BF16),
        pltpu.VMEM((Y - 1, X, B, W), BF16),
        pltpu.VMEM((2, Y - 1, B, W), BF16),
        pltpu.VMEM((2, Y - 1, B, W), BF16),
        pltpu.VMEM((B, p), F32),
        pltpu.VMEM((Z - 1, 8, p), F32),
        pltpu.VMEM((B, p), F32),
        pltpu.VMEM((2, Y, X, B, W), BF16),
        pltpu.VMEM((B, p), F32),
        pltpu.VMEM((2, Y, X, B, W), BF16),
        pltpu.VMEM((Y, R // Y, q), F32),
        pltpu.VMEM((Y // 2, R // Y, q), BF16),
        pltpu.VMEM((Y // 2, R // Y, q), BF16),
        dma((3,)),
        dma((X - 1, Y)), dma((X - 1, Y)),
        dma((Y - 1,)), dma((Y - 1,)),
        dma((2, Y - 1)), dma((2, Y - 1)),
        dma((Z - 1,)), dma((Z - 1,)),
        *gather_sems,
        *gather_sems,
        dma((Y // 2,)), dma((Y // 2,)),
    ]
    return pl.pallas_call(
        functools.partial(kernel, dims),
        out_shape=(
            jax.ShapeDtypeStruct((8, p), BF16),
            jax.ShapeDtypeStruct((R // 2, q), BF16),
        ),
        in_specs=[hbm, hbm, hbm, vmem, vmem, vmem, vmem],
        out_specs=(vmem, vmem),
        scratch_shapes=scratch,
        compiler_params=pltpu.CompilerParams(
            collective_id=0, has_side_effects=True, vmem_limit_bytes=50 * 1024 * 1024
        ),
        name="ladder_step",
    )(mul, integ, amp, slab, slab_amp, rest, divisor)


def solution(mesh, dims=(4, 4, 8)):
    placed = (
        P("op", "vp"),
        P("vp", None),
        P("op", "vp"),
        P("vp", "op"),
        P("vp", "op"),
        P("vp", "op"),
        P("op"),
        P("vp"),
    )
    return jax.shard_map(
        functools.partial(local, dims), mesh=mesh, in_specs=placed,
        out_specs=(P("vp", "op"), P("op", "vp")), check_vma=False,
    )
```

time: 980 us -> 78.5 us (0.08)
  waiting for transfers between devices: 940 us -> 0 us
  Pallas kernels: 0 us -> 69.9 us
  matrix products: 19.5 us -> 0 us
  between operations: 13.8 us -> 0.64 us
    reduce_scatter x2 -> x0, waiting for transfers between devices: 619 us -> none  [the longest x1 599 us: local(): lax.psum_scatter(lax.dot_general(integrals, multipliers, (((0,), (1,)), (...]
    all_gather x2 -> x0, waiting for transfers between devices: 320 us -> none  [the longest x1 211 us: local(): every_new = lax.all_gather(renewed, 'vp', axis=0, tiled=True)]
    pallas_call x0 -> x1, Pallas kernels: none -> 69.9 us  [local(): pl.pallas_call(functools.partial(kernel, dims), out_shape=(jax.ShapeDtype...]
    dot_general x3 -> x0, matrix products: 19.5 us -> none  [the longest x1 7.11 us: local(): jnp.dot(every_amp, multipliers, preferred_element_type=jnp.float32)]
  transfers between devices with their start and end apart: 4 -> 0, of which waited for: 4 -> 0; matrix products, arithmetic and copies ran while one was open for 1% -> 0% of each run, Pallas kernels for 0% -> 0%
where the time goes in v2:
time: 78.5 us; the launch traced here: 77.3 us
  Pallas kernels  69.9 us (89%)
  local copies, waits for them, and re-layouts  5.32 us (7%)
  other arithmetic  1.42 us (2%)
    pallas_call x1, Pallas kernels, local(): pl.pallas_call(functools.partial(kernel, dims), out_shape=(jax.ShapeDtype...  69.9 us
    unnamed x10, local copies, waits for them, and re-layouts  5.32 us

profile of v2, /device:TPU:1, one launch (start us, length us, event | category | flops | bytes accessed | tf_op | source)
XLA Modules:
  0.0 77.3 jit_solution(5453483937435458273)
XLA Ops:
  0.6 0.7 convert_element_type.6
  1.3 0.7 convert_element_type.7
  2.0 0.1 broadcast_subtract_fusion.div_ref
  2.0 0.0 copy-start
  2.0 1.6 %copy-done = bf16[1024,1024]{1,0:T(8,128)(2,1)S(1)} copy-done((bf16[1024,1024]{1,0:T(8,128)(2,1)S(1)}, bf16[1024,1024]{1,0:T(8,128)(2,1)}, u32[]{:S(2)}) %copy-start) | copy-done | bytes 2097176
  3.6 0.0 copy-start.1
  3.6 0.7 copy-done.1
  4.4 0.0 copy-start.2
  4.4 0.7 copy-done.2
  5.1 0.0 copy-start.3
  5.1 0.7 copy-done.3
  5.8 69.9 %ladder_step.1 = (bf16[8,1024]{1,0:T(8,128)(2,1)S(1)}, bf16[512,1024]{1,0:T(8,128)(2,1)S(1)}) custom-call(bf16[1024,1024]{1,0:T(8,128)(2,1)S(1)} %copy-done, bf16[1024,1024]{1,0:T(8,128)(2,1)} %int_hbm.1, bf16[1024,1024]{1,0:T(8,128)(2,1)} %amp_hbm.1, bf16[8,1024]{1,0:T(8,128)(2,1)S(1)} %copy-done.1, bf16[8,1024]{1,0:T(8,128)(2,1)S(1)} %copy-done.2, ...), custom_call_target="tpu_custom_call" | custom-call | tf_op jit(solution)/shard_map/ladder_step/pallas_call | solution.py:354
  75.7 0.6 copy.12
  76.3 1.0 %copy.13 = bf16[512,1024]{1,0:T(8,128)(2,1)} copy(bf16[512,1024]{1,0:T(8,128)(2,1)S(1)} %get-tuple-element.5) | data formatting | bytes 2097152
Async XLA Ops:
  2.0 1.6 %copy-start = (bf16[1024,1024]{1,0:T(8,128)(2,1)S(1)}, bf16[1024,1024]{1,0:T(8,128)(2,1)}, u32[]{:S(2)}) copy-start(bf16[1024,1024]{1,0:T(8,128)(2,1)} %mul_hbm.1) | copy-start | bytes 6291460
  3.6 0.7 copy-start.1
  4.4 0.7 copy-start.2
  5.1 0.7 copy-start.3

commit v3 on v1

v3 whole, which is shorter than its diff:
```python
import functools

import jax
import jax.numpy as jnp
from jax import lax
from jax.experimental import pallas as pl
from jax.experimental.pallas import tpu as pltpu
from jax.sharding import PartitionSpec as P

F32 = jnp.float32
BF16 = jnp.bfloat16
CHUNKS = 4


def kernel(
    dims,
    mul_hbm, int_hbm, amp_hbm, slab_hbm, slab_amp_hbm, rest_hbm, occ_hbm, virt_hbm,
    new_ref, den_ref,
    mul, integ, amp, slab, rest, occ, virt,
    lad, got1, sum1, got2, own3, sum2, got3, new_z, new_all, am_all, acc, swap_out, swap_in,
    load_sem, s1, r1, s2, r2, s3, r3, nz_s, nz_r, n2_s, n2_r, n3_s, n3_r,
    ax_s, ax_r, ay_s, ay_r, az_s, az_r, sw_s, sw_r,
):
    Y, X, Z = dims
    N = Y
    v = lax.axis_index("vp")
    c = lax.axis_index("op")
    y = v // (X * Z)
    x = lax.rem(v // Z, X)
    z = lax.rem(v, Z)
    B = 8 * Z
    R = X * B
    W = lad.shape[-1]
    chunks = lad.shape[0] // 2

    def near(axis, k):
        return lax.rem((y, x, z)[axis] + k, dims[axis])

    def at(axis, i):
        if axis == 0:
            return {"vp": (i * X + x) * Z + z}
        if axis == 1:
            return {"vp": (y * X + i) * Z + z}
        return {"vp": (y * X + x) * Z + i}

    other = {"op": 1 - c}
    sent = []

    def remote(src, dst, ss, rs, device):
        return pltpu.make_async_remote_copy(
            src_ref=src, dst_ref=dst, send_sem=ss, recv_sem=rs,
            device_id=device, device_id_type=pl.DeviceIdType.MESH,
        )

    def send(src, dst, ss, rs, device):
        d = remote(src, dst, ss, rs, device)
        d.start()
        sent.append(d)

    def arrived(ref, ss, rs, device):
        remote(ref, ref, ss, rs, device).wait_recv()

    def post(src, dst, ss, rs, device):
        remote(src, dst, ss, rs, device).start()

    def landed(bulk, ss, rs):
        remote(bulk, bulk, ss, rs, other).wait_recv()

    def left(bulk, ss, rs):
        remote(bulk, bulk, ss, rs, other).wait_send()

    loads = [
        pltpu.make_async_copy(src, dst, load_sem.at[i])
        for i, (src, dst) in enumerate([
            (slab_amp_hbm, am_all.at[z, y, x]), (int_hbm, integ), (mul_hbm, mul),
            (slab_hbm, slab), (rest_hbm, rest), (occ_hbm, occ), (virt_hbm, virt), (amp_hbm, amp),
        ])
    ]
    for d in loads:
        d.start()

    barrier = pltpu.get_barrier_semaphore()
    greet = [at(a, near(a, k)) for a in range(3) for k in range(1, dims[a])] + [other]
    for device in greet:
        pl.semaphore_signal(barrier, inc=1, device_id=device, device_id_type=pl.DeviceIdType.MESH)
    def amp_own():
        mine = am_all.at[z, y, x]
        for k in range(1, X):
            send(mine, mine, ax_s.at[k - 1], ax_r.at[X - 1 - k], at(1, near(1, k)))

    def amp_rows():
        for i in range(X - 1):
            arrived(am_all.at[z, y, near(1, i + 1)], ax_s.at[i], ax_r.at[i], at(1, near(1, i + 1)))
        row = am_all.at[z, y]
        for k in range(1, Y):
            send(row, row, ay_s.at[k - 1], ay_r.at[Y - 1 - k], at(0, near(0, k)))

    H = Z // 2

    def ring_piece(side, step):
        block = near(2, Z - (step - 1)) if side == 0 else near(2, step - 1)
        if step < H:
            return am_all.at[block]
        return am_all.at[block, pl.ds(side * (Y // 2), Y // 2)]

    def ring_landed(side, step):
        block = near(2, Z - step) if side == 0 else near(2, step)
        if step < H:
            return am_all.at[block]
        return am_all.at[block, pl.ds(side * (Y // 2), Y // 2)]

    def ring_wait(step):
        for side in range(2):
            arrived(
                ring_landed(side, step), az_s.at[side, step - 1], az_r.at[side, step - 1],
                at(2, near(2, 1 if side == 0 else Z - 1)),
            )

    def ring_step(step):
        if step == 1:
            for i in range(Y - 1):
                arrived(am_all.at[z, near(0, i + 1)], ay_s.at[i], ay_r.at[i], at(0, near(0, i + 1)))
        else:
            ring_wait(step - 1)
        for side in range(2):
            piece = ring_piece(side, step)
            send(
                piece, piece, az_s.at[side, step - 1], az_r.at[side, step - 1],
                at(2, near(2, 1 if side == 0 else Z - 1)),
            )

    def axes(s):
        return (1, 0) if s % 2 == 0 else (0, 1)

    def ladder(part):
        streams = range(part * chunks, (part + 1) * chunks)
        lo = part * chunks * W
        for n in range(N):
            tile = lax.dot_general(
                integ[:, n * R:(n + 1) * R], mul[lo:lo + chunks * W, :],
                (((0,), (1,)), ((), ())), preferred_element_type=F32,
            )
            for s in streams:
                piece = tile[:, s * W - lo:(s + 1) * W - lo].astype(BF16).reshape(X, B, W)
                if s % 2 == 0:
                    lad[s, :, n] = piece
                else:
                    lad[s, n] = piece

    def ladder_send(chunk):
        for k in (2, 1, 3) if N == 4 else range(1, N):
            for s in (2 * chunk, 2 * chunk + 1):
                one = axes(s)[0]
                j = near(one, k)
                post(lad.at[s, j], got1.at[s, N - 1 - k], s1.at[chunk], r1.at[chunk], at(one, j))

    def sum_first(chunk):
        landed(got1.at[pl.ds(2 * chunk, 2)], s1.at[chunk], r1.at[chunk])
        for s in (2 * chunk + 1, 2 * chunk):
            one, two = axes(s)
            me = (y, x)[one]
            for n in range(N):
                k = n + 1
                b = near(two, k)
                total = lad[s, me, b].astype(F32)
                for i in range(N - 1):
                    total = total + got1[s, i, b].astype(F32)
                if k < N:
                    sum1[s, n] = total.astype(BF16)
                    post(
                        sum1.at[s, n], got2.at[s, N - 1 - k], s2.at[chunk], r2.at[chunk], at(two, b)
                    )
                else:
                    own3[chunk, :, (s % 2) * W:(s % 2 + 1) * W] = total

    def sum_second(chunk):
        landed(got2.at[pl.ds(2 * chunk, 2)], s2.at[chunk], r2.at[chunk])
        for o in range(2):
            s = 2 * chunk + o
            two = axes(s)[1]
            cols = slice(o * W, (o + 1) * W)
            total = own3[chunk, :, cols]
            for i in range(N - 1):
                total = total + got2[s, i].astype(F32)
            own3[chunk, :, cols] = total
            sum2[chunk, :, :, cols] = total.reshape(Z, 8, W).astype(BF16)
        for k in range(1, Z):
            zb = near(2, k)
            post(
                sum2.at[chunk, zb], got3.at[chunk, Z - 1 - k], s3.at[chunk], r3.at[chunk], at(2, zb)
            )

    def renew(chunk):
        cols = slice(chunk * 2 * W, (chunk + 1) * 2 * W)
        landed(got3.at[chunk], s3.at[chunk], r3.at[chunk])
        total = own3[chunk, pl.ds(pl.multiple_of(z * 8, 8), 8), :]
        for i in range(Z - 1):
            total = total + got3[chunk, i].astype(F32)
        row = lax.broadcasted_iota(jnp.int32, (8, 8), 0)
        col = lax.broadcasted_iota(jnp.int32, (8, 8), 1)
        energy = jnp.broadcast_to(virt[...].astype(F32).reshape(1, 8), (8, 8))
        energy = jnp.sum(jnp.where(row == col, energy, 0.0), axis=1, keepdims=True)
        divisor = energy - occ[cols].astype(F32).reshape(1, 2 * W)
        renewed = slab[:, cols].astype(F32) + (total + rest[:, cols].astype(F32)) / divisor
        renewed = renewed.astype(BF16)
        new_ref[:, cols] = renewed
        new_z[chunk, z] = renewed
        here = new_z.at[chunk, z]
        for k in range(1, Z):
            post(here, here, nz_s.at[chunk], nz_r.at[chunk], at(2, near(2, k)))

    def spread_own(chunk):
        landed(got3.at[chunk], nz_s.at[chunk], nz_r.at[chunk])
        whole = new_z[chunk].astype(F32).reshape(B, 2 * W).astype(BF16)
        new_all[y, x, :, chunk * 2 * W:(chunk + 1) * 2 * W] = whole
        for k in (2, 1, 3) if N == 4 else range(1, N):
            for s in (2 * chunk, 2 * chunk + 1):
                two = axes(s)[1]
                here = new_all.at[y, x, :, pl.ds(s * W, W)]
                post(here, here, n2_s.at[chunk], n2_r.at[chunk], at(two, near(two, k)))

    def spread_got(chunk):
        landed(got2.at[pl.ds(2 * chunk, 2)], n2_s.at[chunk], n2_r.at[chunk])
        for k in (2, 1, 3) if N == 4 else range(1, N):
            for s in (2 * chunk, 2 * chunk + 1):
                one = axes(s)[0]
                cols = pl.ds(s * W, W)
                here = new_all.at[:, x, :, cols] if s % 2 == 0 else new_all.at[y, :, :, cols]
                post(here, here, n3_s.at[chunk], n3_r.at[chunk], at(one, near(one, k)))

    def spread_wait(chunk):
        landed(got1.at[pl.ds(2 * chunk, 2)], n3_s.at[chunk], n3_r.at[chunk])

    def all_left(chunk):
        pair = pl.ds(2 * chunk, 2)
        left(got1.at[pair], s1.at[chunk], r1.at[chunk])
        left(got2.at[pair], s2.at[chunk], r2.at[chunk])
        left(got3.at[chunk], s3.at[chunk], r3.at[chunk])
        left(got3.at[chunk], nz_s.at[chunk], nz_r.at[chunk])
        left(got2.at[pair], n2_s.at[chunk], n2_r.at[chunk])

    def amp_part(zb):
        rows = am_all[zb].astype(F32).reshape(Y * X * 8, mul.shape[0]).astype(BF16)
        acc[:, :, zb] = jnp.dot(rows, mul[...], preferred_element_type=F32).reshape(Y, X, 8, acc.shape[-1])

    K = mul.shape[0] // 2

    def product(half, yb):
        left = new_all[yb, :, :, half * K:(half + 1) * K].reshape(R, K)
        return jnp.dot(left, amp[half * K:(half + 1) * K, :], preferred_element_type=F32)

    loads[1].wait()
    loads[2].wait()
    ladder(0)
    loads[0].wait()
    pl.semaphore_wait(barrier, len(greet))
    amp_own()
    ladder_send(0)
    ladder_send(1)
    ladder(1)
    amp_rows()
    sum_first(0)
    ladder_send(2)
    for d in loads[3:]:
        d.wait()
    sum_second(0)
    sum_first(1)
    ladder_send(3)
    ring_step(1)
    renew(0)
    sum_second(1)
    sum_first(2)
    amp_part(z)
    spread_own(0)
    renew(1)
    sum_second(2)
    sum_first(3)
    ring_step(2)
    spread_got(0)
    spread_own(1)
    renew(2)
    sum_second(3)
    amp_part(near(2, 1))
    amp_part(near(2, Z - 1))
    spread_got(1)
    spread_own(2)
    renew(3)
    ring_step(3)
    spread_got(2)
    spread_own(3)
    amp_part(near(2, 2))
    amp_part(near(2, Z - 2))
    spread_got(3)
    ring_step(4)
    amp_part(near(2, 3))
    amp_part(near(2, Z - 3))
    ring_wait(4)
    amp_part(near(2, H))
    for chunk in range(chunks):
        all_left(chunk)
    for chunk in range(chunks // 2):
        spread_wait(chunk)

    @pl.loop(0, Y)
    def _(t):
        acc[t] = acc[t] + product(0, t).reshape(acc.shape[1:])

    for chunk in range(chunks // 2, chunks):
        spread_wait(chunk)
    swaps = []
    for t in range(Y // 2):
        yb = (1 - c) * (Y // 2) + t
        swap_out[t] = (acc[yb].reshape(R, acc.shape[-1]) + product(1, yb)).astype(BF16)
        d = remote(swap_out.at[t], swap_in.at[t], sw_s.at[t], sw_r.at[t], other)
        d.start()
        swaps.append(d)
    for t in range(Y // 2):
        yb = c * (Y // 2) + t
        mine_t = acc[yb].reshape(R, acc.shape[-1]) + product(1, yb)
        swaps[t].wait_recv()
        den_ref[pl.ds(t * R, R), :] = (mine_t + swap_in[t].astype(F32)).astype(BF16)
    for chunk in range(chunks):
        left(got1.at[pl.ds(2 * chunk, 2)], n3_s.at[chunk], n3_r.at[chunk])
    for d in sent + swaps:
        d.wait_send()


def local(dims, mul, integ, amp, slab, slab_amp, rest, occupied, virtual):
    Y, X, Z = dims
    N = Y
    B = 8 * Z
    R = Y * X * B
    C = CHUNKS
    S = 2 * C
    p, q = mul.shape
    W = p // S
    dma = pltpu.SemaphoreType.DMA
    vmem = pl.BlockSpec(memory_space=pltpu.VMEM)
    hbm = pl.BlockSpec(memory_space=pltpu.HBM)
    scratch = [
        pltpu.VMEM((p, q), BF16),
        pltpu.VMEM((q, R), BF16),
        pltpu.VMEM((p, q), BF16),
        pltpu.VMEM((8, p), BF16),
        pltpu.VMEM((8, p), BF16),
        pltpu.VMEM((p,), BF16),
        pltpu.VMEM((8,), BF16),
        pltpu.VMEM((S, Y, X, B, W), BF16),
        pltpu.VMEM((S, N - 1, N, B, W), BF16),
        pltpu.VMEM((S, N - 1, B, W), BF16),
        pltpu.VMEM((S, N - 1, B, W), BF16),
        pltpu.VMEM((C, B, 2 * W), F32),
        pltpu.VMEM((C, Z, 8, 2 * W), BF16),
        pltpu.VMEM((C, Z - 1, 8, 2 * W), BF16),
        pltpu.VMEM((C, Z, 8, 2 * W), BF16),
        pltpu.VMEM((Y, X, B, p), BF16),
        pltpu.VMEM((Z, Y, X, 8, p), BF16),
        pltpu.VMEM((Y, X, Z, 8, q), F32),
        pltpu.VMEM((Y // 2, R // Y, q), BF16),
        pltpu.VMEM((Y // 2, R // Y, q), BF16),
        dma((8,)),
        *[dma((C,)) for _ in range(12)],
        dma((X - 1,)), dma((X - 1,)),
        dma((Y - 1,)), dma((Y - 1,)),
        dma((2, Z // 2)), dma((2, Z // 2)),
        dma((Y // 2,)), dma((Y // 2,)),
    ]
    return pl.pallas_call(
        functools.partial(kernel, dims),
        out_shape=(
            jax.ShapeDtypeStruct((8, p), BF16),
            jax.ShapeDtypeStruct((R // 2, q), BF16),
        ),
        in_specs=[hbm] * 8,
        out_specs=(vmem, vmem),
        scratch_shapes=scratch,
        compiler_params=pltpu.CompilerParams(
            collective_id=0, has_side_effects=True, vmem_limit_bytes=50 * 1024 * 1024
        ),
        name="ladder_step",
    )(*[pltpu.with_memory_space_constraint(a, pltpu.HBM) for a in (mul, integ, amp, slab, slab_amp, rest, occupied, virtual)])


def solution(mesh, dims=(4, 4, 8)):
    placed = (
        P("op", "vp"),
        P("vp", None),
        P("op", "vp"),
        P("vp", "op"),
        P("vp", "op"),
        P("vp", "op"),
        P("op"),
        P("vp"),
    )
    return jax.shard_map(
        functools.partial(local, dims), mesh=mesh, in_specs=placed,
        out_specs=(P("vp", "op"), P("op", "vp")), check_vma=False,
    )
```

time: 980 us -> 68.5 us (0.07)
  waiting for transfers between devices: 940 us -> 0 us
  Pallas kernels: 0 us -> 66.2 us
  matrix products: 19.5 us -> 0 us
  between operations: 13.8 us -> 0.64 us
    reduce_scatter x2 -> x0, waiting for transfers between devices: 619 us -> none  [the longest x1 599 us: local(): lax.psum_scatter(lax.dot_general(integrals, multipliers, (((0,), (1,)), (...]
    all_gather x2 -> x0, waiting for transfers between devices: 320 us -> none  [the longest x1 211 us: local(): every_new = lax.all_gather(renewed, 'vp', axis=0, tiled=True)]
    pallas_call x0 -> x1, Pallas kernels: none -> 66.2 us  [local(): pl.pallas_call(functools.partial(kernel, dims), out_shape=(jax.ShapeDtype...]
    dot_general x3 -> x0, matrix products: 19.5 us -> none  [the longest x1 7.11 us: local(): jnp.dot(every_amp, multipliers, preferred_element_type=jnp.float32)]
  transfers between devices with their start and end apart: 4 -> 0, of which waited for: 4 -> 0; matrix products, arithmetic and copies ran while one was open for 1% -> 0% of each run, Pallas kernels for 0% -> 0%
where the time goes in v3:
time: 68.5 us; the launch traced here: 68.4 us
  Pallas kernels  66.2 us (97%)
  local copies, waits for them, and re-layouts  1.58 us (2%)
    pallas_call x1, Pallas kernels, local(): pl.pallas_call(functools.partial(kernel, dims), out_shape=(jax.ShapeDtype...  66.2 us
    unnamed x2, local copies, waits for them, and re-layouts  1.58 us

profile of v3, /device:TPU:1, one launch (start us, length us, event | category | flops | bytes accessed | tf_op | source)
XLA Modules:
  0.0 68.4 jit_solution(4077285883174001748)
XLA Ops:
  0.6 66.2 %ladder_step.1 = (bf16[8,1024]{1,0:T(8,128)(2,1)S(1)}, bf16[512,1024]{1,0:T(8,128)(2,1)S(1)}) custom-call(bf16[1024,1024]{1,0:T(8,128)(2,1)} %mul_hbm.1, bf16[1024,1024]{1,0:T(8,128)(2,1)} %int_hbm.1, bf16[1024,1024]{1,0:T(8,128)(2,1)} %amp_hbm.1, bf16[8,1024]{1,0:T(8,128)(2,1)} %slab_hbm.1, bf16[8,1024]{1,0:T(8,128)(2,1)} %slab_amp_hbm.1, ...), custom_call_target="tpu_custom_call" | custom-call | tf_op jit(solution)/shard_map/ladder_step/pallas_call | solution.py:368
  66.8 0.6 copy.12
  67.4 1.0 %copy.13 = bf16[512,1024]{1,0:T(8,128)(2,1)} copy(bf16[512,1024]{1,0:T(8,128)(2,1)S(1)} %get-tuple-element.5) | data formatting | bytes 2097152

commit v4 on v3

--- a/solution.py
+++ b/solution.py
@@ -17,9 +17,10 @@
     mul_hbm, int_hbm, amp_hbm, slab_hbm, slab_amp_hbm, rest_hbm, occ_hbm, virt_hbm,
     new_ref, den_ref,
     mul, integ, amp, slab, rest, occ, virt,
-    lad, got1, sum1, got2, own3, sum2, got3, new_z, new_all, am_all, acc, swap_out, swap_in,
+    lad, got1, sum1, got2, own3, sum2, got3, new_z, new_all, am_all, am_z, am_full, acc,
+    swap_out, swap_in,
     load_sem, s1, r1, s2, r2, s3, r3, nz_s, nz_r, n2_s, n2_r, n3_s, n3_r,
-    ax_s, ax_r, ay_s, ay_r, az_s, az_r, sw_s, sw_r,
+    ax_s, ax_r, ay_s, ay_r, az_s, az_r, ag_s, ag_r, sw_s, sw_r,
 ):
     Y, X, Z = dims
     N = Y
@@ -32,6 +33,8 @@
     R = X * B
     W = lad.shape[-1]
     chunks = lad.shape[0] // 2
+    A = am_z.shape[-1]
+    V = A // 2
 
     def near(axis, k):
         return lax.rem((y, x, z)[axis] + k, dims[axis])
@@ -72,7 +75,9 @@
     loads = [
         pltpu.make_async_copy(src, dst, load_sem.at[i])
         for i, (src, dst) in enumerate([
-            (slab_amp_hbm, am_all.at[z, y, x]), (int_hbm, integ), (mul_hbm, mul),
+            (slab_amp_hbm.at[:, pl.ds(A, mul.shape[0] - A)], am_all.at[z, y, x]),
+            (int_hbm, integ), (mul_hbm, mul),
+            (slab_amp_hbm.at[:, pl.ds(0, A)], am_z.at[z]),
             (slab_hbm, slab), (rest_hbm, rest), (occ_hbm, occ), (virt_hbm, virt), (amp_hbm, amp),
         ])
     ]
@@ -153,6 +158,10 @@
                 one = axes(s)[0]
                 j = near(one, k)
                 post(lad.at[s, j], got1.at[s, N - 1 - k], s1.at[chunk], r1.at[chunk], at(one, j))
+
+    def ladder_next(chunk):
+        left(got1.at[pl.ds(2 * chunk, 2)], s1.at[chunk], r1.at[chunk])
+        ladder_send(chunk + 1)
 
     def sum_first(chunk):
         landed(got1.at[pl.ds(2 * chunk, 2)], s1.at[chunk], r1.at[chunk])
@@ -233,15 +242,43 @@
 
     def all_left(chunk):
         pair = pl.ds(2 * chunk, 2)
-        left(got1.at[pair], s1.at[chunk], r1.at[chunk])
+        if chunk == chunks - 1:
+            left(got1.at[pair], s1.at[chunk], r1.at[chunk])
         left(got2.at[pair], s2.at[chunk], r2.at[chunk])
         left(got3.at[chunk], s3.at[chunk], r3.at[chunk])
         left(got3.at[chunk], nz_s.at[chunk], nz_r.at[chunk])
         left(got2.at[pair], n2_s.at[chunk], n2_r.at[chunk])
 
+    def staged_z():
+        here = am_z.at[z]
+        for k in range(1, Z):
+            post(here, here, ag_s.at[0], ag_r.at[0], at(2, near(2, k)))
+
+    def staged_own():
+        landed(am_z.at[pl.ds(0, Z - 1)], ag_s.at[0], ag_r.at[0])
+        am_full[y, x] = am_z[...].astype(F32).reshape(B, A).astype(BF16)
+        for k in range(1, N):
+            for o in range(2):
+                here = am_full.at[y, x, :, pl.ds(o * V, V)]
+                post(here, here, ag_s.at[1], ag_r.at[1], at(axes(o)[1], near(axes(o)[1], k)))
+
+    def staged_got():
+        landed(am_full.at[0, pl.ds(0, N - 1)], ag_s.at[1], ag_r.at[1])
+        for k in range(1, N):
+            for o in range(2):
+                cols = pl.ds(o * V, V)
+                here = am_full.at[:, x, :, cols] if o == 0 else am_full.at[y, :, :, cols]
+                post(here, here, ag_s.at[2], ag_r.at[2], at(axes(o)[0], near(axes(o)[0], k)))
+
+    def staged_wait():
+        landed(am_full.at[pl.ds(0, N - 1)], ag_s.at[2], ag_r.at[2])
+        left(am_z.at[pl.ds(0, Z - 1)], ag_s.at[0], ag_r.at[0])
+        left(am_full.at[0, pl.ds(0, N - 1)], ag_s.at[1], ag_r.at[1])
+        left(am_full.at[pl.ds(0, N - 1)], ag_s.at[2], ag_r.at[2])
+
     def amp_part(zb):
-        rows = am_all[zb].astype(F32).reshape(Y * X * 8, mul.shape[0]).astype(BF16)
-        acc[:, :, zb] = jnp.dot(rows, mul[...], preferred_element_type=F32).reshape(Y, X, 8, acc.shape[-1])
+        rows = am_all[zb].astype(F32).reshape(Y * X * 8, mul.shape[0] - A).astype(BF16)
+        acc[:, :, zb] = jnp.dot(rows, mul[A:, :], preferred_element_type=F32).reshape(Y, X, 8, acc.shape[-1])
 
     K = mul.shape[0] // 2
 
@@ -253,49 +290,54 @@
     loads[2].wait()
     ladder(0)
     loads[0].wait()
+    loads[3].wait()
     pl.semaphore_wait(barrier, len(greet))
     amp_own()
+    staged_z()
     ladder_send(0)
-    ladder_send(1)
     ladder(1)
+    ladder_next(0)
     amp_rows()
+    for d in loads[4:]:
+        d.wait()
     sum_first(0)
-    ladder_send(2)
-    for d in loads[3:]:
-        d.wait()
+    ladder_next(1)
+    staged_own()
+    sum_first(1)
+    ladder_next(2)
+    ring_step(1)
     sum_second(0)
-    sum_first(1)
-    ladder_send(3)
-    ring_step(1)
+    sum_first(2)
+    sum_second(1)
+    sum_first(3)
+    staged_got()
+    amp_part(z)
     renew(0)
-    sum_second(1)
-    sum_first(2)
-    amp_part(z)
-    spread_own(0)
+    sum_second(2)
+    ring_step(2)
     renew(1)
-    sum_second(2)
-    sum_first(3)
-    ring_step(2)
-    spread_got(0)
-    spread_own(1)
-    renew(2)
     sum_second(3)
     amp_part(near(2, 1))
     amp_part(near(2, Z - 1))
-    spread_got(1)
-    spread_own(2)
+    spread_own(0)
+    renew(2)
+    ring_step(3)
+    spread_own(1)
     renew(3)
-    ring_step(3)
-    spread_got(2)
-    spread_own(3)
+    spread_got(0)
     amp_part(near(2, 2))
     amp_part(near(2, Z - 2))
-    spread_got(3)
+    spread_own(2)
+    spread_got(1)
     ring_step(4)
+    spread_own(3)
+    spread_got(2)
     amp_part(near(2, 3))
     amp_part(near(2, Z - 3))
+    spread_got(3)
     ring_wait(4)
     amp_part(near(2, H))
+    staged_wait()
     for chunk in range(chunks):
         all_left(chunk)
     for chunk in range(chunks // 2):
@@ -303,7 +345,8 @@
 
     @pl.loop(0, Y)
     def _(t):
-        acc[t] = acc[t] + product(0, t).reshape(acc.shape[1:])
+        staged = jnp.dot(am_full[t].reshape(R, A), mul[:A, :], preferred_element_type=F32)
+        acc[t] = acc[t] + (product(0, t) + staged).reshape(acc.shape[1:])
 
     for chunk in range(chunks // 2, chunks):
         spread_wait(chunk)
@@ -334,6 +377,7 @@
     S = 2 * C
     p, q = mul.shape
     W = p // S
+    A = p // 2
     dma = pltpu.SemaphoreType.DMA
     vmem = pl.BlockSpec(memory_space=pltpu.VMEM)
     hbm = pl.BlockSpec(memory_space=pltpu.HBM)
@@ -354,15 +398,18 @@
         pltpu.VMEM((C, Z - 1, 8, 2 * W), BF16),
         pltpu.VMEM((C, Z, 8, 2 * W), BF16),
         pltpu.VMEM((Y, X, B, p), BF16),
-        pltpu.VMEM((Z, Y, X, 8, p), BF16),
+        pltpu.VMEM((Z, Y, X, 8, p - A), BF16),
+        pltpu.VMEM((Z, 8, A), BF16),
+        pltpu.VMEM((Y, X, B, A), BF16),
         pltpu.VMEM((Y, X, Z, 8, q), F32),
         pltpu.VMEM((Y // 2, R // Y, q), BF16),
         pltpu.VMEM((Y // 2, R // Y, q), BF16),
-        dma((8,)),
+        dma((9,)),
         *[dma((C,)) for _ in range(12)],
         dma((X - 1,)), dma((X - 1,)),
         dma((Y - 1,)), dma((Y - 1,)),
         dma((2, Z // 2)), dma((2, Z // 2)),
+        dma((3,)), dma((3,)),
         dma((Y // 2,)), dma((Y // 2,)),
     ]
     return pl.pallas_call(

time: 68.5 us -> 60.4 us (0.88)
  Pallas kernels: 66.2 us -> 58.1 us
    pallas_call x1, Pallas kernels: 66.2 us -> 58.1 us  [local(): pl.pallas_call(functools.partial(kernel, dims), out_shape=(jax.ShapeDtype...]
where the time goes in v4:
time: 60.4 us; the launch traced here: 60.3 us
  Pallas kernels  58.1 us (96%)
  local copies, waits for them, and re-layouts  1.58 us (3%)
  between operations  0.64 us (1%)
    pallas_call x1, Pallas kernels, local(): pl.pallas_call(functools.partial(kernel, dims), out_shape=(jax.ShapeDtype...  58.1 us
    unnamed x2, local copies, waits for them, and re-layouts  1.58 us

profile of v4, /device:TPU:1, one launch (start us, length us, event | category | flops | bytes accessed | tf_op | source)
XLA Modules:
  0.0 60.3 jit_solution(6046087982805327798)
XLA Ops:
  0.6 58.1 %ladder_step.1 = (bf16[8,1024]{1,0:T(8,128)(2,1)S(1)}, bf16[512,1024]{1,0:T(8,128)(2,1)S(1)}) custom-call(bf16[1024,1024]{1,0:T(8,128)(2,1)} %mul_hbm.1, bf16[1024,1024]{1,0:T(8,128)(2,1)} %int_hbm.1, bf16[1024,1024]{1,0:T(8,128)(2,1)} %amp_hbm.1, bf16[8,1024]{1,0:T(8,128)(2,1)} %slab_hbm.1, bf16[8,1024]{1,0:T(8,128)(2,1)} %slab_amp_hbm.1, ...), custom_call_target="tpu_custom_call" | custom-call | tf_op jit(solution)/shard_map/ladder_step/pallas_call | solution.py:415
  58.7 0.6 %copy.12 = bf16[8,1024]{1,0:T(8,128)(2,1)} copy(bf16[8,1024]{1,0:T(8,128)(2,1)S(1)} %get-tuple-element.4) | data formatting | bytes 32768
  59.3 1.0 %copy.13 = bf16[512,1024]{1,0:T(8,128)(2,1)} copy(bf16[512,1024]{1,0:T(8,128)(2,1)S(1)} %get-tuple-element.5) | data formatting | bytes 2097152

commit v5 on v4

--- a/solution.py
+++ b/solution.py
@@ -47,6 +47,10 @@
         return {"vp": (y * X + x) * Z + i}
 
     other = {"op": 1 - c}
+
+    def far_first(n):
+        return sorted(range(1, n), key=lambda k: -min(k, n - k))
+
     sent = []
 
     def remote(src, dst, ss, rs, device):
@@ -153,7 +157,7 @@
                     lad[s, n] = piece
 
     def ladder_send(chunk):
-        for k in (2, 1, 3) if N == 4 else range(1, N):
+        for k in far_first(N):
             for s in (2 * chunk, 2 * chunk + 1):
                 one = axes(s)[0]
                 j = near(one, k)
@@ -168,8 +172,8 @@
         for s in (2 * chunk + 1, 2 * chunk):
             one, two = axes(s)
             me = (y, x)[one]
-            for n in range(N):
-                k = n + 1
+            for k in far_first(N) + [N]:
+                n = k - 1
                 b = near(two, k)
                 total = lad[s, me, b].astype(F32)
                 for i in range(N - 1):
@@ -193,7 +197,7 @@
                 total = total + got2[s, i].astype(F32)
             own3[chunk, :, cols] = total
             sum2[chunk, :, :, cols] = total.reshape(Z, 8, W).astype(BF16)
-        for k in range(1, Z):
+        for k in far_first(Z):
             zb = near(2, k)
             post(
                 sum2.at[chunk, zb], got3.at[chunk, Z - 1 - k], s3.at[chunk], r3.at[chunk], at(2, zb)
@@ -215,27 +219,34 @@
         new_ref[:, cols] = renewed
         new_z[chunk, z] = renewed
         here = new_z.at[chunk, z]
-        for k in range(1, Z):
+        for k in far_first(Z):
             post(here, here, nz_s.at[chunk], nz_r.at[chunk], at(2, near(2, k)))
 
     def spread_own(chunk):
         landed(got3.at[chunk], nz_s.at[chunk], nz_r.at[chunk])
         whole = new_z[chunk].astype(F32).reshape(B, 2 * W).astype(BF16)
         new_all[y, x, :, chunk * 2 * W:(chunk + 1) * 2 * W] = whole
-        for k in (2, 1, 3) if N == 4 else range(1, N):
+        for k in far_first(N):
             for s in (2 * chunk, 2 * chunk + 1):
                 two = axes(s)[1]
                 here = new_all.at[y, x, :, pl.ds(s * W, W)]
                 post(here, here, n2_s.at[chunk], n2_r.at[chunk], at(two, near(two, k)))
+        for k in far_first(N):
+            for s in (2 * chunk, 2 * chunk + 1):
+                one = axes(s)[0]
+                here = new_all.at[y, x, :, pl.ds(s * W, W)]
+                post(here, here, n3_s.at[chunk], n3_r.at[chunk], at(one, near(one, k)))
 
     def spread_got(chunk):
         landed(got2.at[pl.ds(2 * chunk, 2)], n2_s.at[chunk], n2_r.at[chunk])
-        for k in (2, 1, 3) if N == 4 else range(1, N):
-            for s in (2 * chunk, 2 * chunk + 1):
-                one = axes(s)[0]
-                cols = pl.ds(s * W, W)
-                here = new_all.at[:, x, :, cols] if s % 2 == 0 else new_all.at[y, :, :, cols]
-                post(here, here, n3_s.at[chunk], n3_r.at[chunk], at(one, near(one, k)))
+        for k in far_first(N):
+            for i in far_first(N):
+                for s in (2 * chunk, 2 * chunk + 1):
+                    one, two = axes(s)
+                    cols = pl.ds(s * W, W)
+                    b = near(two, i)
+                    here = new_all.at[b, x, :, cols] if s % 2 == 0 else new_all.at[y, b, :, cols]
+                    post(here, here, n3_s.at[chunk], n3_r.at[chunk], at(one, near(one, k)))
 
     def spread_wait(chunk):
         landed(got1.at[pl.ds(2 * chunk, 2)], n3_s.at[chunk], n3_r.at[chunk])
@@ -251,7 +262,7 @@
 
     def staged_z():
         here = am_z.at[z]
-        for k in range(1, Z):
+        for k in far_first(Z):
             post(here, here, ag_s.at[0], ag_r.at[0], at(2, near(2, k)))
 
     def staged_own():
@@ -302,39 +313,36 @@
         d.wait()
     sum_first(0)
     ladder_next(1)
-    staged_own()
     sum_first(1)
     ladder_next(2)
+    staged_own()
     ring_step(1)
     sum_second(0)
     sum_first(2)
     sum_second(1)
     sum_first(3)
-    staged_got()
-    amp_part(z)
     renew(0)
     sum_second(2)
+    staged_got()
     ring_step(2)
     renew(1)
     sum_second(3)
-    amp_part(near(2, 1))
-    amp_part(near(2, Z - 1))
     spread_own(0)
     renew(2)
     ring_step(3)
     spread_own(1)
     renew(3)
     spread_got(0)
-    amp_part(near(2, 2))
-    amp_part(near(2, Z - 2))
     spread_own(2)
     spread_got(1)
     ring_step(4)
     spread_own(3)
     spread_got(2)
-    amp_part(near(2, 3))
-    amp_part(near(2, Z - 3))
     spread_got(3)
+    amp_part(z)
+    for k in range(1, H):
+        amp_part(near(2, k))
+        amp_part(near(2, Z - k))
     ring_wait(4)
     amp_part(near(2, H))
     staged_wait()

time: 60.4 us -> 59.1 us (0.978)
  Pallas kernels: 58.1 us -> 56.8 us
    pallas_call x1, Pallas kernels: 58.1 us -> 56.8 us  [local(): pl.pallas_call(functools.partial(kernel, dims), out_shape=(jax.ShapeDtype...]
where the time goes in v5:
time: 59.1 us
  Pallas kernels  56.8 us (96%)
  local copies, waits for them, and re-layouts  1.58 us (3%)
  between operations  0.64 us (1%)
    pallas_call x1, Pallas kernels, local(): pl.pallas_call(functools.partial(kernel, dims), out_shape=(jax.ShapeDtype...  56.8 us
    unnamed x2, local copies, waits for them, and re-layouts  1.58 us

profile of v5, /device:TPU:1, one launch (start us, length us, event | category | flops | bytes accessed | tf_op | source)
XLA Modules:
  0.0 59.1 jit_solution(1918960211274625856)
XLA Ops:
  0.6 56.8 %ladder_step.1 = (bf16[8,1024]{1,0:T(8,128)(2,1)S(1)}, bf16[512,1024]{1,0:T(8,128)(2,1)S(1)}) custom-call(bf16[1024,1024]{1,0:T(8,128)(2,1)} %mul_hbm.1, bf16[1024,1024]{1,0:T(8,128)(2,1)} %int_hbm.1, bf16[1024,1024]{1,0:T(8,128)(2,1)} %amp_hbm.1, bf16[8,1024]{1,0:T(8,128)(2,1)} %slab_hbm.1, bf16[8,1024]{1,0:T(8,128)(2,1)} %slab_amp_hbm.1, ...), custom_call_target="tpu_custom_call" | custom-call | tf_op jit(solution)/shard_map/ladder_step/pallas_call | solution.py:423
  57.5 0.6 %copy.12 = bf16[8,1024]{1,0:T(8,128)(2,1)} copy(bf16[8,1024]{1,0:T(8,128)(2,1)S(1)} %get-tuple-element.4) | data formatting | bytes 32768
  58.1 1.0 %copy.13 = bf16[512,1024]{1,0:T(8,128)(2,1)} copy(bf16[512,1024]{1,0:T(8,128)(2,1)S(1)} %get-tuple-element.5) | data formatting | bytes 2097152

commit v6 on v5

--- a/solution.py
+++ b/solution.py
@@ -359,17 +359,26 @@
     for chunk in range(chunks // 2, chunks):
         spread_wait(chunk)
     swaps = []
-    for t in range(Y // 2):
-        yb = (1 - c) * (Y // 2) + t
-        swap_out[t] = (acc[yb].reshape(R, acc.shape[-1]) + product(1, yb)).astype(BF16)
+    half = X // 2
+    D = half * B
+
+    def final_rows(core, t):
+        yb = core * (Y // 2) + t // 2
+        xs = slice((t % 2) * half, (t % 2 + 1) * half)
+        left_rows = new_all[yb, xs, :, K:].reshape(D, K)
+        return acc[yb, xs].reshape(D, acc.shape[-1]) + jnp.dot(
+            left_rows, amp[K:, :], preferred_element_type=F32
+        )
+
+    for t in range(Y):
+        swap_out[t] = final_rows(1 - c, t).astype(BF16)
         d = remote(swap_out.at[t], swap_in.at[t], sw_s.at[t], sw_r.at[t], other)
         d.start()
         swaps.append(d)
-    for t in range(Y // 2):
-        yb = c * (Y // 2) + t
-        mine_t = acc[yb].reshape(R, acc.shape[-1]) + product(1, yb)
+    for t in range(Y):
+        mine_t = final_rows(c, t)
         swaps[t].wait_recv()
-        den_ref[pl.ds(t * R, R), :] = (mine_t + swap_in[t].astype(F32)).astype(BF16)
+        den_ref[pl.ds(t * D, D), :] = (mine_t + swap_in[t].astype(F32)).astype(BF16)
     for chunk in range(chunks):
         left(got1.at[pl.ds(2 * chunk, 2)], n3_s.at[chunk], n3_r.at[chunk])
     for d in sent + swaps:
@@ -410,15 +419,15 @@
         pltpu.VMEM((Z, 8, A), BF16),
         pltpu.VMEM((Y, X, B, A), BF16),
         pltpu.VMEM((Y, X, Z, 8, q), F32),
-        pltpu.VMEM((Y // 2, R // Y, q), BF16),
-        pltpu.VMEM((Y // 2, R // Y, q), BF16),
+        pltpu.VMEM((Y, R // Y // 2, q), BF16),
+        pltpu.VMEM((Y, R // Y // 2, q), BF16),
         dma((9,)),
         *[dma((C,)) for _ in range(12)],
         dma((X - 1,)), dma((X - 1,)),
         dma((Y - 1,)), dma((Y - 1,)),
         dma((2, Z // 2)), dma((2, Z // 2)),
         dma((3,)), dma((3,)),
-        dma((Y // 2,)), dma((Y // 2,)),
+        dma((Y,)), dma((Y,)),
     ]
     return pl.pallas_call(
         functools.partial(kernel, dims),

time: 59.1 us -> 59.1 us (level)
  no operation moved by 1% of the time
where the time goes in v6:
time: 59.1 us; the launch traced here: 59 us
  Pallas kernels  56.8 us (96%)
  local copies, waits for them, and re-layouts  1.58 us (3%)
  between operations  0.64 us (1%)
    pallas_call x1, Pallas kernels, local(): pl.pallas_call(functools.partial(kernel, dims), out_shape=(jax.ShapeDtype...  56.8 us
    unnamed x2, local copies, waits for them, and re-layouts  1.58 us

profile of v6, /device:TPU:1, one launch (start us, length us, event | category | flops | bytes accessed | tf_op | source)
XLA Modules:
  0.0 59.0 jit_solution(12992304030066421153)
XLA Ops:
  0.6 56.8 %ladder_step.1 = (bf16[8,1024]{1,0:T(8,128)(2,1)S(1)}, bf16[512,1024]{1,0:T(8,128)(2,1)S(1)}) custom-call(bf16[1024,1024]{1,0:T(8,128)(2,1)} %mul_hbm.1, bf16[1024,1024]{1,0:T(8,128)(2,1)} %int_hbm.1, bf16[1024,1024]{1,0:T(8,128)(2,1)} %amp_hbm.1, bf16[8,1024]{1,0:T(8,128)(2,1)} %slab_hbm.1, bf16[8,1024]{1,0:T(8,128)(2,1)} %slab_amp_hbm.1, ...), custom_call_target="tpu_custom_call" | custom-call | tf_op jit(solution)/shard_map/ladder_step/pallas_call | solution.py:432
  57.4 0.6 %copy.12 = bf16[8,1024]{1,0:T(8,128)(2,1)} copy(bf16[8,1024]{1,0:T(8,128)(2,1)S(1)} %get-tuple-element.4) | data formatting | bytes 32768
  58.0 1.0 %copy.13 = bf16[512,1024]{1,0:T(8,128)(2,1)} copy(bf16[512,1024]{1,0:T(8,128)(2,1)S(1)} %get-tuple-element.5) | data formatting | bytes 2097152
